TPU v7x, 128 devices: a whole 4x4x4 slice. The times are simulated.
128 devices in a mesh: gx: 8 (over z, core), gy: 4 (over x), gz: 4 (over y).
Axes of the slice: x: 4, y: 4, z: 4, core: 2. Of those that a mesh axis runs over, the one named last changes fastest.
Arguments:
- source_residual: float32 [64, 256, 1024], P('gz', 'gx', 'gy'), may hold values from -8 to 8
- storage: float32 [64, 256, 1024], P('gz', 'gx', 'gy'), may hold values from 0.05 to 3
- conductivity: float32 [64, 256, 1024], P('gz', 'gx', 'gy'), may hold values from 0.05 to 2
- primal_label: int32 [64, 256, 4], P('gz', 'gx', 'gy'), may hold values from 0 to 31
- zone_of_block: int32 [16384, 1], P(('gx', 'gy', 'gz')), may hold values from 0 to 127; in each aligned block of 128 rows (0 to 127, 128 to 255, ...) at most 4 rows name the same one
- coarse_factor: float32 [4096, 4096], P(('gx', 'gy', 'gz')), may hold values from -0.0009765625 to 0.0009765625
- zone_factor: bfloat16 [128, 256, 256], P(('gx', 'gy', 'gz')), may hold values from -0.375 to 0.375
Outputs:
- solution: float32 [64, 256, 1024], P('gz', 'gx', 'gy')
- residual: float32 [64, 256, 1024], P('gz', 'gx', 'gy')
Inputs may be any that keep to these rules, and one draw needn't show every extreme that they name: `zone_of_block`: among the face blocks of one subdomain, no zone is named more than 4 times.
All inputs are finite; a program needn't handle non-finite values.
Results may differ from a plain program's by a relative error of at most 0.018.
Values may be sent and summed in bfloat16 or wider, within the bound.
No kernel may reach another device: no remote copies, remote signals or barrier semaphores. Data moves between devices by JAX's collectives and lax.ppermute only.
A program may use at most 64 MiB of HBM per device.

v0:
```python
import jax
import jax.numpy as jnp
from jax import lax
from jax.sharding import PartitionSpec as P

FB = 256
KC = 32
INNER = 8
ITERS = 2
CAP = 4
HIGHEST = lax.Precision.HIGHEST


def padded_2(block, sides, width):
    for axis, dim in sides:
        count = lax.axis_size(axis)
        forward = [(i, i + 1) for i in range(count - 1)]
        backward = [(target, source) for source, target in forward]
        low = lax.ppermute(
            lax.slice_in_dim(block, block.shape[dim] - width, None, axis=dim), axis, forward
        )
        high = lax.ppermute(lax.slice_in_dim(block, 0, width, axis=dim), axis, backward)
        block = jnp.concatenate([low, block, high], axis=dim)
    return block


def neighbour_sum(conductances, padded):
    summed = conductances[0] * padded[2:, 1:-1, 1:-1] + conductances[1] * padded[:-2, 1:-1, 1:-1]
    summed = (
        summed
        + conductances[2] * padded[1:-1, 2:, 1:-1]
        + conductances[3] * padded[1:-1, :-2, 1:-1]
    )
    summed = (
        summed
        + conductances[4] * padded[1:-1, 1:-1, 2:]
        + conductances[5] * padded[1:-1, 1:-1, :-2]
    )
    return summed


def face_conductances(conductivity):
    padded = padded_2(conductivity, (("gx", 1), ("gy", 2), ("gz", 0)), 1)
    return (
        0.5 * (padded[2:, 1:-1, 1:-1] + conductivity),
        0.5 * (padded[:-2, 1:-1, 1:-1] + conductivity),
        0.5 * (padded[1:-1, 2:, 1:-1] + conductivity),
        0.5 * (padded[1:-1, :-2, 1:-1] + conductivity),
        0.5 * (padded[1:-1, 1:-1, 2:] + conductivity),
        0.5 * (padded[1:-1, 1:-1, :-2] + conductivity),
    )


def apply_global(field, conductances, diagonal):
    padded = padded_2(field.astype(jnp.bfloat16), (("gx", 1), ("gy", 2), ("gz", 0)), 1).astype(
        field.dtype
    )
    return diagonal * field - neighbour_sum(conductances, padded)


def local_solve(rhs, conductances, diagonal):
    iterate = jnp.zeros_like(rhs)
    remain = rhs
    scaled = remain / diagonal
    search = scaled
    inner_rz = jnp.sum(remain * scaled)
    for sweep_index in range(INNER):
        applied = diagonal * search - neighbour_sum(conductances, jnp.pad(search, 1))
        step_size = inner_rz / jnp.sum(search * applied)
        iterate = iterate + step_size * search
        remain = remain - step_size * applied
        scaled = remain / diagonal
        inner_next = jnp.sum(remain * scaled)
        search = scaled + inner_next / inner_rz * search
        inner_rz = inner_next
    return iterate


def dispatch_table(zone_of_block, zone_count):
    zone_vec = zone_of_block[:, 0]
    hits = (zone_vec[:, None] == jnp.arange(zone_count, dtype=jnp.int32)[None, :]).astype(jnp.int32)
    before = jnp.cumsum(hits, axis=0) - hits
    slot_of = jnp.sum(before * hits, axis=1)
    slot_hits = (slot_of[:, None] == jnp.arange(CAP, dtype=jnp.int32)[None, :]).astype(jnp.int32)
    dispatch = hits[:, :, None] * slot_hits[:, None, :]
    return dispatch.reshape(zone_vec.shape[0], zone_count * CAP).astype(jnp.bfloat16)


def lift_return(received, factor):
    lifted = jnp.einsum("sif,fg->sig", received, factor, preferred_element_type=jnp.float32).astype(
        jnp.bfloat16
    )
    return jnp.einsum("sig,fg->sif", lifted, factor, preferred_element_type=jnp.float32).astype(
        jnp.bfloat16
    )


def per_device(
    source_residual, storage, conductivity, primal_label, zone_of_block, coarse_factor, zone_factor
):
    conductances = face_conductances(conductivity)
    diagonal = (
        storage
        + conductances[0]
        + conductances[1]
        + conductances[2]
        + conductances[3]
        + conductances[4]
        + conductances[5]
    )
    onehot = (primal_label.reshape(-1)[:, None] == jnp.arange(KC, dtype=jnp.int32)[None, :]).astype(
        jnp.float32
    )
    zone_count = lax.axis_size(("gx", "gy", "gz"))
    dispatch = dispatch_table(zone_of_block, zone_count)
    factor = zone_factor[0]
    cells_z, cells_x, cells_y = source_residual.shape

    def refine_term(field):
        layers = jnp.concatenate([field[:2], field[-2:]], axis=0)
        blocks = layers.reshape(-1, FB).astype(jnp.bfloat16)
        outgoing = jnp.einsum(
            "bs,bf->sf", dispatch, blocks, preferred_element_type=jnp.float32
        ).astype(jnp.bfloat16)
        outgoing = outgoing.reshape(zone_count, CAP, FB)
        returned = lax.all_to_all(
            lift_return(
                lax.all_to_all(
                    outgoing, ("gx", "gy", "gz"), split_axis=0, concat_axis=0, tiled=True
                ),
                factor,
            ),
            ("gx", "gy", "gz"),
            split_axis=0,
            concat_axis=0,
            tiled=True,
        )
        returned = returned.reshape(zone_count * CAP, FB)
        placed = jnp.dot(dispatch, returned, preferred_element_type=jnp.float32)
        placed = placed.reshape(4, cells_x, cells_y)
        middle = jnp.zeros((cells_z - 4, cells_x, cells_y), jnp.float32)
        return jnp.concatenate([placed[:2], middle, placed[2:]], axis=0)

    def coarse_partial(field):
        line_values = jnp.sum(field, axis=2).reshape(-1)
        restricted = jnp.dot(line_values, onehot, precision=HIGHEST)
        return jnp.dot(restricted, coarse_factor, precision=HIGHEST)

    def coarse_vector(field):
        return lax.psum(coarse_partial(field), ("gx", "gy", "gz"))

    def product_sum(value):
        return lax.psum(value, ("gx", "gy", "gz"))

    def precondition(field, summed):
        coarse_coef = jnp.dot(coarse_factor, summed, precision=HIGHEST)
        line_values = jnp.dot(onehot, coarse_coef, precision=HIGHEST).reshape(cells_z, cells_x, 1)
        return local_solve(field, conductances, diagonal) + line_values + refine_term(field)

    solution = jnp.zeros_like(source_residual)
    residual = source_residual
    summed = coarse_vector(residual)
    precond = precondition(residual, summed)
    current_rz = product_sum(jnp.sum(residual * precond))
    direction = precond
    for outer_step in range(ITERS):
        applied = apply_global(direction, conductances, diagonal)
        final_step = outer_step + 1 == ITERS
        curvature = lax.psum(jnp.sum(direction * applied), ("gx", "gy", "gz"))
        step_size = current_rz / curvature
        solution = solution + step_size * direction
        residual = residual - step_size * applied
        if not final_step:
            summed = coarse_vector(residual)
            precond = precondition(residual, summed)
            next_rz = product_sum(jnp.sum(residual * precond))
            direction = precond + next_rz / current_rz * direction
            current_rz = next_rz
    return (solution, residual)


def solution(mesh):
    in_specs = (
        P("gz", "gx", "gy"),
        P("gz", "gx", "gy"),
        P("gz", "gx", "gy"),
        P("gz", "gx", "gy"),
        P(("gx", "gy", "gz"), None),
        P(("gx", "gy", "gz"), None),
        P(("gx", "gy", "gz"), None, None),
    )
    out_specs = (P("gz", "gx", "gy"), P("gz", "gx", "gy"))
    return jax.shard_map(
        per_device, mesh=mesh, in_specs=in_specs, out_specs=out_specs, check_vma=False
    )
```

profile of v0, /device:TPU:1, one launch (start us, length us, event | category | flops | bytes accessed | tf_op | source)
XLA Modules:
  0.0 639.4 jit_solution(13267346616168054444)
XLA Ops:
  1.7 3.3 collective-permute-start.1
  5.0 3.5 collective-permute-start
  11.7 3.1 collective-permute-start.2
  16.2 5.5 collective-permute-done.2
  21.8 4.1 collective-permute-done.3
  27.3 4.6 collective-permute-start.5
  33.5 2.4 fusion.261
  35.9 2.3 fusion.241
  39.0 66.3 %psum.42 = f32[4096]{0:T(1024)S(1)} all-reduce(f32[4096]{0:T(1024)S(1)} %bitcast.65), channel_id=1, replica_groups=mesh['gx'=8,'gy'=4,'gz'=4] {'gx','gy','gz'}, use_global_device_ids=true, to_apply=%region_17.18 | all-reduce | flops 4096 | bytes 32768 | tf_op jit(solution)/shard_map/psum | solution.py:150
  107.6 3.2 multiply_reduce_fusion.31
  115.5 6.6 %all-to-all-start = ((bf16[128,4,256]{2,1,0:T(4,128)(2,1)}), bf16[128,4,256]{2,1,0:T(4,128)(2,1)}, u32[]{:S(2)}, u32[]{:S(2)}) async-start(bf16[128,4,256]{2,1,0:T(4,128)(2,1)} %reshape.106), calls=%async_computation | async-start | bytes 524288 | tf_op jit(solution)/shard_map/all_to_all | solution.py:128
  123.5 2.2 multiply_reduce_fusion.30
  127.0 2.9 multiply_reduce_fusion.29
  132.6 2.2 multiply_reduce_fusion.28
  136.1 2.9 multiply_reduce_fusion.27
  141.7 2.2 multiply_reduce_fusion.26
  145.2 2.9 multiply_reduce_fusion.25
  150.7 2.2 multiply_reduce_fusion.24
  154.0 2.9 multiply_reduce_fusion.23
  159.5 2.2 multiply_reduce_fusion.22
  163.0 2.9 multiply_reduce_fusion.21
  168.6 2.2 multiply_reduce_fusion.20
  175.3 2.3 multiply_add_fusion.9
  177.6 2.2 convolution_convert_fusion.3
  181.7 10.2 %all-to-all-start.1 = ((bf16[128,4,256]{2,1,0:T(4,128)(2,1)}), bf16[128,4,256]{2,1,0:T(4,128)(2,1)}, u32[]{:S(2)}, u32[]{:S(2)}) async-start(bf16[128,4,256]{2,1,0:T(4,128)(2,1)} %copy.23), calls=%async_computation.1 | async-start | bytes 524288 | tf_op jit(solution)/shard_map/all_to_all | solution.py:126
  191.9 3.9 fusion.219
  197.1 5.6 all-to-all-done.1
  203.9 2.6 fusion.253
  206.6 3.1 collective-permute-start.6
  211.7 3.1 collective-permute-done.7
  215.1 2.2 collective-permute-start.8
  219.8 4.3 collective-permute-done.9
  224.2 2.3 collective-permute-start.10
  227.8 3.8 collective-permute-done.11
  232.0 2.4 multiply_reduce_fusion.17
  234.4 73.4 %all-reduce.16 = (f32[]{:T(128)}, f32[]{:T(128)}) all-reduce(f32[]{:T(128)} %get-tuple-element.6, f32[]{:T(128)} %get-tuple-element.5), channel_id=1, replica_groups=mesh['gx'=8,'gy'=4,'gz'=4] {'gx','gy','gz'}, use_global_device_ids=true, to_apply=%region_21.22 | all-reduce | flops 2 | bytes 16 | tf_op jit(solution)/shard_map/psum | solution.py:153
  310.6 2.3 fusion.240
  313.6 64.2 %psum.45 = f32[4096]{0:T(1024)S(1)} all-reduce(f32[4096]{0:T(1024)S(1)} %bitcast.67), channel_id=1, replica_groups=mesh['gx'=8,'gy'=4,'gz'=4] {'gx','gy','gz'}, use_global_device_ids=true, to_apply=%region_41.42 | all-reduce | flops 4096 | bytes 32768 | tf_op jit(solution)/shard_map/psum | solution.py:150
  379.9 3.1 multiply_reduce_fusion.14
  387.7 5.5 all-to-all-start.2
  394.6 2.2 multiply_reduce_fusion.13
  398.0 2.9 multiply_reduce_fusion.12
  403.4 2.1 multiply_reduce_fusion.11
  406.7 2.9 multiply_reduce_fusion.10
  412.2 2.1 multiply_reduce_fusion.9
  415.6 3.0 multiply_reduce_fusion.8
  421.2 2.2 multiply_reduce_fusion.7
  424.6 3.0 multiply_reduce_fusion.6
  430.2 2.2 multiply_reduce_fusion.5
  433.8 3.0 multiply_reduce_fusion.4
  439.5 2.2 multiply_reduce_fusion.3
  446.3 2.4 multiply_add_fusion.2
  452.6 10.4 %all-to-all-start.3 = ((bf16[128,4,256]{2,1,0:T(4,128)(2,1)}), bf16[128,4,256]{2,1,0:T(4,128)(2,1)}, u32[]{:S(2)}, u32[]{:S(2)}) async-start(bf16[128,4,256]{2,1,0:T(4,128)(2,1)} %copy.27), calls=%async_computation.3 | async-start | bytes 524288 | tf_op jit(solution)/shard_map/all_to_all | solution.py:126
  463.0 3.8 fusion.218
  468.1 5.7 all-to-all-done.3
  475.0 4.2 multiply_reduce_fusion.1
  479.2 62.7 %psum.46 = f32[]{:T(128)} all-reduce(f32[]{:T(128)} %get-tuple-element.16), channel_id=1, replica_groups=mesh['gx'=8,'gy'=4,'gz'=4] {'gx','gy','gz'}, use_global_device_ids=true, to_apply=%region_43.44 | all-reduce | flops 1 | bytes 8 | tf_op jit(solution)/shard_map/psum | solution.py:153
  544.5 3.3 collective-permute-start.12
  549.7 3.1 collective-permute-done.13
  557.3 4.2 collective-permute-done.15
  565.0 3.6 collective-permute-done.17
  569.1 2.2 multiply_reduce_fusion
  571.3 63.8 %psum.47 = f32[]{:T(128)} all-reduce(f32[]{:T(128)} %get-tuple-element.12), channel_id=1, replica_groups=mesh['gx'=8,'gy'=4,'gz'=4] {'gx','gy','gz'}, use_global_device_ids=true, to_apply=%region_45.46 | all-reduce | flops 1 | bytes 8 | tf_op jit(solution)/shard_map/psum | solution.py:169
  636.4 2.7 multiply_subtract_fusion
  (177 shorter events, 66.5 us)
Async XLA Ops:
  0.6 38.0 %copy-start = (f32[32,4096]{1,0:T(8,128)S(1)}, f32[32,4096]{1,0:T(8,128)}, u32[]{:S(2)}) copy-start(f32[32,4096]{1,0:T(8,128)} %param.12) | copy-start | bytes 1572868
  1.7 8.6 %collective-permute-start.1 = (f32[16,1,256]{2,1,0:T(1,128)S(1)}, f32[16,1,256]{2,1,0:T(1,128)S(1)}, u32[]{:S(2)}, u32[]{:S(2)}) collective-permute-start(f32[16,1,256]{2,1,0:T(1,128)S(1)} %get-tuple-element.101), channel_id=1, source_target_pairs={{16,0},{32,16},{48,32},{64,48},{80,64},{96,80},{112,96},{17,1},{33... | collective-permute-start | bytes 49160 | tf_op jit(solution)/shard_map/ppermute | solution.py:22
  5.0 5.3 collective-permute-start
  10.3 15.6 %copy-start.1 = (f32[16,32,256]{2,1,0:T(8,128)S(1)}, f32[16,32,256]{2,1,0:T(8,128)}, u32[]{:S(2)}) copy-start(f32[16,32,256]{2,1,0:T(8,128)} %param.9) | copy-start | bytes 1572868
  11.7 20.9 %copy-start.41 = (s32[16,32,1]{1,2,0:T(1,128)S(1)}, s32[16,32,1]{1,2,0:T(1,128)}, u32[]{:S(2)}) copy-start(s32[16,32,1]{1,2,0:T(1,128)} %param.10) | copy-start | bytes 6148
  11.7 10.1 %collective-permute-start.2 = (f32[16,34,1]{2,1,0:T(8,128)S(1)}, f32[16,34,1]{2,1,0:T(8,128)S(1)}, u32[]{:S(2)}, u32[]{:S(2)}) collective-permute-start(f32[16,34,1]{2,1,0:T(8,128)S(1)} %get-tuple-element.93), channel_id=1, source_target_pairs={{0,4},{4,8},{8,12},{1,5},{5,9},{9,13},{2,6},{6,10},{10,14},{3,7},{... | collective-permute-start | bytes 6536 | tf_op jit(solution)/shard_map/ppermute | solution.py:19
  14.8 11.0 %collective-permute-start.3 = (f32[16,34,1]{2,1,0:T(8,128)S(1)}, f32[16,34,1]{2,1,0:T(8,128)S(1)}, u32[]{:S(2)}, u32[]{:S(2)}) collective-permute-start(f32[16,34,1]{2,1,0:T(8,128)S(1)} %get-tuple-element.94), channel_id=1, source_target_pairs={{4,0},{8,4},{12,8},{5,1},{9,5},{13,9},{6,2},{10,6},{14,10},{7,3},{... | collective-permute-start | bytes 6536 | tf_op jit(solution)/shard_map/ppermute | solution.py:22
  21.8 11.7 %copy-start.39 = (f32[16,34,1]{2,1,0:T(8,128)}, f32[16,34,1]{2,1,0:T(8,128)S(1)}, u32[]{:S(2)}) copy-start(f32[16,34,1]{2,1,0:T(8,128)S(1)} %collective-permute-done.2) | copy-start | bytes 6532
  25.9 7.6 %copy-start.40 = (f32[16,34,1]{2,1,0:T(8,128)}, f32[16,34,1]{2,1,0:T(8,128)S(1)}, u32[]{:S(2)}) copy-start(f32[16,34,1]{2,1,0:T(8,128)S(1)} %collective-permute-done.3) | copy-start | bytes 6532
  26.0 7.5 %collective-permute-start.4 = (f32[1,34,258]{2,1,0:T(8,128)S(1)}, f32[1,34,258]{2,1,0:T(8,128)S(1)}, u32[]{:S(2)}, u32[]{:S(2)}) collective-permute-start(f32[1,34,258]{2,1,0:T(8,128)S(1)} %get-tuple-element.91), channel_id=1, source_target_pairs={{1,0},{2,1},{3,2},{5,4},{6,5},{7,6},{9,8},{10,9},{11,10},{13,12},{... | collective-permute-start | bytes 105272 | tf_op jit(solution)/shard_map/ppermute | solution.py:22
  27.3 6.2 collective-permute-start.5
  33.5 2.5 copy-start.20
  35.9 2.3 copy-start.2
  35.9 2.3 copy-start.37
  115.5 62.1 %all-to-all-start = ((bf16[128,4,256]{2,1,0:T(4,128)(2,1)}), bf16[128,4,256]{2,1,0:T(4,128)(2,1)}, u32[]{:S(2)}, u32[]{:S(2)}) async-start(bf16[128,4,256]{2,1,0:T(4,128)(2,1)} %reshape.106), calls=%async_computation | async-start | bytes 524288 | tf_op jit(solution)/shard_map/all_to_all | solution.py:128
  122.1 1.4 copy-start.3
  123.5 2.2 copy-start.26
  131.2 1.4 copy-start.4
  132.6 2.2 copy-start.28
  140.3 1.4 copy-start.5
  141.7 2.2 copy-start.30
  149.3 1.4 copy-start.6
  150.6 2.2 copy-start.32
  158.1 1.4 copy-start.7
  159.5 2.2 copy-start.34
  167.2 1.4 copy-start.8
  168.5 2.2 copy-start.23
  181.7 21.0 %all-to-all-start.1 = ((bf16[128,4,256]{2,1,0:T(4,128)(2,1)}), bf16[128,4,256]{2,1,0:T(4,128)(2,1)}, u32[]{:S(2)}, u32[]{:S(2)}) async-start(bf16[128,4,256]{2,1,0:T(4,128)(2,1)} %copy.23), calls=%async_computation.1 | async-start | bytes 524288 | tf_op jit(solution)/shard_map/all_to_all | solution.py:126
  202.7 1.2 copy-start.24
  206.6 25.4 %copy-start.35 = (f32[16,32,256]{2,1,0:T(8,128)}, f32[16,32,256]{2,1,0:T(8,128)S(1)}, u32[]{:S(2)}) copy-start(f32[16,32,256]{2,1,0:T(8,128)S(1)} %get-tuple-element.53) | copy-start | bytes 1572868
  206.6 5.1 collective-permute-start.6
  209.8 5.1 collective-permute-start.7
  215.1 4.7 collective-permute-start.8
  217.3 14.7 %copy-start.9 = (f32[16,32,256]{2,1,0:T(8,128)S(1)}, f32[16,32,256]{2,1,0:T(8,128)}, u32[]{:S(2)}) copy-start(f32[16,32,256]{2,1,0:T(8,128)} %copy-done.2) | copy-start | bytes 1572868
  217.3 14.7 %copy-start.21 = (f32[16,32,256]{2,1,0:T(8,128)S(1)}, f32[16,32,256]{2,1,0:T(8,128)}, u32[]{:S(2)}) copy-start(f32[16,32,256]{2,1,0:T(8,128)} %param.7) | copy-start | bytes 1572868
  217.3 6.7 %collective-permute-start.9 = (bf16[16,34,1]{2,1,0:T(8,128)(2,1)S(1)}, bf16[16,34,1]{2,1,0:T(8,128)(2,1)S(1)}, u32[]{:S(2)}, u32[]{:S(2)}) collective-permute-start(bf16[16,34,1]{2,1,0:T(8,128)(2,1)S(1)} %get-tuple-element.106), channel_id=1, source_target_pairs={{4,0},{8,4},{12,8},{5,1},{9,5},{13,9},{6,2},{10,6},{14,10},{7,3},{... | collective-permute-start | bytes 3272 | tf_op jit(solution)/shard_map/ppermute | solution.py:22
  224.2 3.6 collective-permute-start.10
  226.4 5.1 collective-permute-start.11
  309.1 1.4 copy-start.10
  310.5 2.3 copy-start.18
  310.6 2.3 copy-start.36
  387.7 61.0 %all-to-all-start.2 = ((bf16[128,4,256]{2,1,0:T(4,128)(2,1)}), bf16[128,4,256]{2,1,0:T(4,128)(2,1)}, u32[]{:S(2)}, u32[]{:S(2)}) async-start(bf16[128,4,256]{2,1,0:T(4,128)(2,1)} %reshape.108), calls=%async_computation.2 | async-start | bytes 524288 | tf_op jit(solution)/shard_map/all_to_all | solution.py:128
  393.2 1.4 copy-start.11
  394.6 2.2 copy-start.25
  402.0 1.4 copy-start.12
  403.4 2.1 copy-start.27
  410.8 1.4 copy-start.13
  412.2 2.2 copy-start.29
  419.8 1.4 copy-start.14
  421.2 2.2 copy-start.31
  428.9 1.4 copy-start.15
  430.2 2.2 copy-start.33
  438.1 1.4 copy-start.16
  439.5 2.2 copy-start.22
  446.3 2.4 copy-start.42
  452.6 21.2 %all-to-all-start.3 = ((bf16[128,4,256]{2,1,0:T(4,128)(2,1)}), bf16[128,4,256]{2,1,0:T(4,128)(2,1)}, u32[]{:S(2)}, u32[]{:S(2)}) async-start(bf16[128,4,256]{2,1,0:T(4,128)(2,1)} %copy.27), calls=%async_computation.3 | async-start | bytes 524288 | tf_op jit(solution)/shard_map/all_to_all | solution.py:126
  544.5 24.6 %copy-start.38 = (f32[16,32,256]{2,1,0:T(8,128)}, f32[16,32,256]{2,1,0:T(8,128)S(1)}, u32[]{:S(2)}) copy-start(f32[16,32,256]{2,1,0:T(8,128)S(1)} %get-tuple-element.15) | copy-start | bytes 1572868
  544.5 5.2 collective-permute-start.12
  547.8 5.1 collective-permute-start.13
  553.1 4.1 collective-permute-start.14
  554.5 14.6 %copy-start.17 = (f32[16,32,256]{2,1,0:T(8,128)S(1)}, f32[16,32,256]{2,1,0:T(8,128)}, u32[]{:S(2)}) copy-start(f32[16,32,256]{2,1,0:T(8,128)} %copy-done.2) | copy-start | bytes 1572868
  554.5 7.0 %collective-permute-start.15 = (bf16[16,34,1]{2,1,0:T(8,128)(2,1)S(1)}, bf16[16,34,1]{2,1,0:T(8,128)(2,1)S(1)}, u32[]{:S(2)}, u32[]{:S(2)}) collective-permute-start(bf16[16,34,1]{2,1,0:T(8,128)(2,1)S(1)} %get-tuple-element.104), channel_id=1, source_target_pairs={{4,0},{8,4},{12,8},{5,1},{9,5},{13,9},{6,2},{10,6},{14,10},{7,3},{... | collective-permute-start | bytes 3272 | tf_op jit(solution)/shard_map/ppermute | solution.py:22
  561.6 3.4 collective-permute-start.16
  563.5 5.1 collective-permute-start.17
  (1 other events, 1.2 us)
where the time goes:
time: 647 us; the launch traced here: 639 us
  blocking collectives  330 us (51%)
  other arithmetic  123 us (19%)
  starting transfers between devices  73.5 us (11%)
  waiting for transfers between devices  45.4 us (7%)
  between operations  43.5 us (7%)
  local copies, waits for them, and re-layouts  11.7 us (2%)
  matrix products  11.4 us (2%)
    psum x2, blocking collectives, product_sum(): return lax.psum(value, ('gx', 'gy', 'gz'))  136 us
    psum x2, blocking collectives, coarse_vector(): return lax.psum(coarse_partial(field), ('gx', 'gy', 'gz'))  131 us
    psum x1, blocking collectives, per_device(): curvature = lax.psum(jnp.sum(direction * applied), ('gx', 'gy', 'gz'))  63.8 us
    reduce_sum x14, other arithmetic, local_solve(): inner_next = jnp.sum(remain * scaled)  39.8 us
    reduce_sum x14, other arithmetic, local_solve(): step_size = inner_rz / jnp.sum(search * applied)  33.9 us
    ppermute x9, waiting for transfers between devices, padded_2(): lax.ppermute(lax.slice_in_dim(block, 0, width, axis=dim), axis, backward)  26.2 us
    ppermute x9, starting transfers between devices, padded_2(): lax.ppermute(lax.slice_in_dim(block, block.shape[dim] - width, None, axis...  25.4 us
    add x14, other arithmetic, local_solve(): search = scaled + inner_next / inner_rz * search  20.8 us
  transfers between devices with their start and end apart: 22, of which 12 were waited for; matrix products, arithmetic and copies ran while one was open for 14% of the time, Pallas kernels for 0%

commit v1 on v0

--- a/solution.py
+++ b/solution.py
@@ -150,7 +150,7 @@
         return lax.psum(coarse_partial(field), ("gx", "gy", "gz"))
 
     def product_sum(value):
-        return lax.psum(value, ("gx", "gy", "gz"))
+        return jnp.sum(lax.all_gather(value, ("gx", "gy", "gz")), axis=0)
 
     def precondition(field, summed):
         coarse_coef = jnp.dot(coarse_factor, summed, precision=HIGHEST)

time: 647 us -> 649 us (level)
  starting transfers between devices: 73.5 us -> 89.9 us
  waiting for transfers between devices: 45.4 us -> 31.9 us
    psum x2 -> x0, blocking collectives: 136 us -> none  [product_sum(): return lax.psum(value, ('gx', 'gy', 'gz'))]
    unnamed x0 -> x2, blocking collectives: none -> 127 us
    ppermute x9, starting transfers between devices: 25.4 us -> 46.2 us  [padded_2(): lax.ppermute(lax.slice_in_dim(block, block.shape[dim] - width, None, axis...]
    ppermute x9, waiting for transfers between devices: 26.2 us -> 14 us  [padded_2(): lax.ppermute(lax.slice_in_dim(block, 0, width, axis=dim), axis, backward)]
    all_to_all x2, starting transfers between devices: 20.6 us -> 10.5 us  [refine_term(): lax.all_to_all(lift_return(lax.all_to_all(outgoing, ('gx', 'gy', 'gz'), s...]
  transfers between devices with their start and end apart: 22 -> 22, of which waited for: 12 -> 13; matrix products, arithmetic and copies ran while one was open for 14% -> 15% of each run, Pallas kernels for 0% -> 0%
where the time goes in v1:
time: 649 us; the launch traced here: 642 us
  blocking collectives  326 us (50%)
  other arithmetic  128 us (20%)
  starting transfers between devices  89.9 us (14%)
  between operations  44.8 us (7%)
  waiting for transfers between devices  31.9 us (5%)
  local copies, waits for them, and re-layouts  10.9 us (2%)
  matrix products  10.7 us (2%)
    psum x2, blocking collectives, coarse_vector(): return lax.psum(coarse_partial(field), ('gx', 'gy', 'gz'))  135 us
    unnamed x2, blocking collectives  127 us
    psum x1, blocking collectives, per_device(): curvature = lax.psum(jnp.sum(direction * applied), ('gx', 'gy', 'gz'))  65 us
    ppermute x9, starting transfers between devices, padded_2(): lax.ppermute(lax.slice_in_dim(block, block.shape[dim] - width, None, axis...  46.2 us
    reduce_sum x14, other arithmetic, local_solve(): inner_next = jnp.sum(remain * scaled)  40 us
    reduce_sum x14, other arithmetic, local_solve(): step_size = inner_rz / jnp.sum(search * applied)  33.9 us
    add x14, other arithmetic, local_solve(): search = scaled + inner_next / inner_rz * search  20.8 us
    all_to_all x2, starting transfers between devices, refine_term(): lax.all_to_all(outgoing, ('gx', 'gy', 'gz'), split_axis=0, concat_axis=0,...  18.1 us
  transfers between devices with their start and end apart: 22, of which 13 were waited for; matrix products, arithmetic and copies ran while one was open for 15% of the time, Pallas kernels for 0%

profile of v1, /device:TPU:1, one launch (start us, length us, event | category | flops | bytes accessed | tf_op | source)
XLA Modules:
  0.0 642.2 jit_solution(2108157409736343637)
XLA Ops:
  1.7 4.9 collective-permute-start
  14.3 4.0 collective-permute-start.2
  18.4 4.4 collective-permute-done.3
  24.7 3.2 collective-permute-start.5
  30.9 2.8 collective-permute-done.4
  33.7 2.3 fusion.261
  36.1 2.3 fusion.241
  39.8 3.1 multiply_reduce_fusion.31
  45.6 13.0 %all-to-all-start = ((bf16[128,4,256]{2,1,0:T(4,128)(2,1)}), bf16[128,4,256]{2,1,0:T(4,128)(2,1)}, u32[]{:S(2)}, u32[]{:S(2)}) async-start(bf16[128,4,256]{2,1,0:T(4,128)(2,1)} %reshape.106), calls=%async_computation | async-start | bytes 524288 | tf_op jit(solution)/shard_map/all_to_all | solution.py:128
  59.4 67.7 %psum.28 = f32[4096]{0:T(1024)S(1)} all-reduce(f32[4096]{0:T(1024)S(1)} %bitcast.67), channel_id=1, replica_groups=mesh['gx'=8,'gy'=4,'gz'=4] {'gx','gy','gz'}, use_global_device_ids=true, to_apply=%region_17.18 | all-reduce | flops 4096 | bytes 32768 | tf_op jit(solution)/shard_map/psum | solution.py:150
  130.6 2.2 multiply_reduce_fusion.30
  134.2 3.0 multiply_reduce_fusion.29
  139.9 2.2 multiply_reduce_fusion.28
  143.4 2.9 multiply_reduce_fusion.27
  149.0 2.2 multiply_reduce_fusion.26
  152.5 3.0 multiply_reduce_fusion.25
  158.2 2.2 multiply_reduce_fusion.24
  161.7 2.9 multiply_reduce_fusion.23
  167.3 2.2 multiply_reduce_fusion.22
  170.9 2.9 multiply_reduce_fusion.21
  176.4 2.2 multiply_reduce_fusion.20
  183.1 2.4 multiply_add_fusion.9
  185.5 2.1 convolution_convert_fusion.3
  189.4 5.3 all-to-all-start.1
  194.7 3.9 fusion.219
  199.9 5.7 all-to-all-done.1
  206.9 3.4 fusion.253
  210.3 2.7 collective-permute-start.7
  213.0 2.9 collective-permute-start.6
  218.3 4.0 collective-permute-start.8
  222.3 2.8 collective-permute-done.9
  228.1 16.0 %collective-permute-start.10 = (bf16[1,34,258]{2,1,0:T(8,128)(2,1)}, bf16[1,34,258]{2,1,0:T(8,128)(2,1)S(1)}, u32[]{:S(2)}, u32[]{:S(2)}) collective-permute-start(bf16[1,34,258]{2,1,0:T(8,128)(2,1)} %get-tuple-element.97), channel_id=1, source_target_pairs={{0,1},{1,2},{2,3},{4,5},{5,6},{6,7},{8,9},{9,10},{10,11},{12,13},{... | collective-permute-start | bytes 52640 | tf_op jit(solution)/shard_map/ppermute | solution.py:19
  245.7 2.4 multiply_reduce_fusion.17
  248.9 63.9 %all-reduce.18 = (f32[128]{0:T(128)S(1)}, f32[]{:T(128)}) all-reduce(f32[128]{0:T(128)S(1)} %dynamic-update-slice, f32[]{:T(128)} %get-tuple-element.5), channel_id=1, replica_groups=mesh['gx'=8,'gy'=4,'gz'=4] {'gx','gy','gz'}, use_global_device_ids=true, to_apply=%add.16 | all-reduce | flops 129 | bytes 1032
  316.1 2.3 fusion.240
  319.7 3.2 multiply_reduce_fusion.14
  323.9 5.1 all-to-all-start.2
  329.8 67.3 %psum.30 = f32[4096]{0:T(1024)S(1)} all-reduce(f32[4096]{0:T(1024)S(1)} %bitcast.69), channel_id=1, replica_groups=mesh['gx'=8,'gy'=4,'gz'=4] {'gx','gy','gz'}, use_global_device_ids=true, to_apply=%region_41.42 | all-reduce | flops 4096 | bytes 32768 | tf_op jit(solution)/shard_map/psum | solution.py:150
  400.6 2.2 multiply_reduce_fusion.13
  404.1 3.0 multiply_reduce_fusion.12
  409.8 2.2 multiply_reduce_fusion.11
  413.2 3.0 multiply_reduce_fusion.10
  418.9 2.2 multiply_reduce_fusion.9
  422.4 3.0 multiply_reduce_fusion.8
  428.0 2.2 multiply_reduce_fusion.7
  431.5 3.0 multiply_reduce_fusion.6
  437.1 2.2 multiply_reduce_fusion.5
  440.6 3.0 multiply_reduce_fusion.4
  446.3 2.2 multiply_reduce_fusion.3
  453.0 2.4 multiply_add_fusion.2
  455.4 2.1 convolution_convert_fusion
  459.3 5.3 all-to-all-start.3
  464.6 3.8 fusion.218
  469.7 5.9 all-to-all-done.3
  476.8 4.3 multiply_reduce_fusion.1
  481.9 62.7 %all-reduce.17 = f32[128]{0:T(128)S(1)} all-reduce(f32[128]{0:T(128)S(1)} %dynamic-update-slice.1), channel_id=1, replica_groups=mesh['gx'=8,'gy'=4,'gz'=4] {'gx','gy','gz'}, use_global_device_ids=true, to_apply=%add.17 | all-reduce | flops 128 | bytes 1024
  547.9 2.7 collective-permute-start.13
  550.6 3.0 collective-permute-start.12
  555.9 4.1 collective-permute-start.14
  560.0 2.6 collective-permute-done.15
  565.1 4.0 collective-permute-start.16
  570.6 2.3 multiply_reduce_fusion
  572.9 65.0 %psum.31 = f32[]{:T(128)} all-reduce(f32[]{:T(128)} %get-tuple-element.12), channel_id=1, replica_groups=mesh['gx'=8,'gy'=4,'gz'=4] {'gx','gy','gz'}, use_global_device_ids=true, to_apply=%region_45.46 | all-reduce | flops 1 | bytes 8 | tf_op jit(solution)/shard_map/psum | solution.py:169
  639.2 2.7 multiply_subtract_fusion
  (195 shorter events, 65.4 us)
Async XLA Ops:
  0.6 58.4 %copy-start = (f32[32,4096]{1,0:T(8,128)S(1)}, f32[32,4096]{1,0:T(8,128)}, u32[]{:S(2)}) copy-start(f32[32,4096]{1,0:T(8,128)} %param.12) | copy-start | bytes 1572868
  1.7 8.6 %collective-permute-start = (f32[16,1,256]{2,1,0:T(1,128)S(1)}, f32[16,1,256]{2,1,0:T(1,128)S(1)}, u32[]{:S(2)}, u32[]{:S(2)}) collective-permute-start(f32[16,1,256]{2,1,0:T(1,128)S(1)} %get-tuple-element.102), channel_id=1, source_target_pairs={{0,16},{16,32},{32,48},{48,64},{64,80},{80,96},{96,112},{1,17},{17... | collective-permute-start | bytes 49160 | tf_op jit(solution)/shard_map/ppermute | solution.py:19
  6.6 5.1 collective-permute-start.1
  10.3 14.2 %copy-start.1 = (f32[16,32,256]{2,1,0:T(8,128)S(1)}, f32[16,32,256]{2,1,0:T(8,128)}, u32[]{:S(2)}) copy-start(f32[16,32,256]{2,1,0:T(8,128)} %param.9) | copy-start | bytes 1572868
  13.0 17.1 %copy-start.47 = (s32[16,32,1]{1,2,0:T(1,128)S(1)}, s32[16,32,1]{1,2,0:T(1,128)}, u32[]{:S(2)}) copy-start(s32[16,32,1]{1,2,0:T(1,128)} %param.10) | copy-start | bytes 6148
  13.0 9.8 %collective-permute-start.3 = (f32[16,34,1]{2,1,0:T(8,128)S(1)}, f32[16,34,1]{2,1,0:T(8,128)S(1)}, u32[]{:S(2)}, u32[]{:S(2)}) collective-permute-start(f32[16,34,1]{2,1,0:T(8,128)S(1)} %get-tuple-element.94), channel_id=1, source_target_pairs={{4,0},{8,4},{12,8},{5,1},{9,5},{13,9},{6,2},{10,6},{14,10},{7,3},{... | collective-permute-start | bytes 6536 | tf_op jit(solution)/shard_map/ppermute | solution.py:22
  14.3 10.3 %collective-permute-start.2 = (f32[16,34,1]{2,1,0:T(8,128)S(1)}, f32[16,34,1]{2,1,0:T(8,128)S(1)}, u32[]{:S(2)}, u32[]{:S(2)}) collective-permute-start(f32[16,34,1]{2,1,0:T(8,128)S(1)} %get-tuple-element.93), channel_id=1, source_target_pairs={{0,4},{4,8},{8,12},{1,5},{5,9},{9,13},{2,6},{6,10},{10,14},{3,7},{... | collective-permute-start | bytes 6536 | tf_op jit(solution)/shard_map/ppermute | solution.py:19
  22.8 8.1 %copy-start.41 = (f32[16,34,1]{2,1,0:T(8,128)}, f32[16,34,1]{2,1,0:T(8,128)S(1)}, u32[]{:S(2)}) copy-start(f32[16,34,1]{2,1,0:T(8,128)S(1)} %collective-permute-done.3) | copy-start | bytes 6532
  24.6 6.3 copy-start.42
  24.7 6.2 collective-permute-start.5
  27.9 5.8 collective-permute-start.4
  29.3 13.7 %copy-start.39 = (bf16[128,128,4]{0,2,1:T(4,128)(2,1)}, bf16[128,128,4]{0,2,1:T(4,128)(2,1)S(1)}, u32[]{:S(2)}) copy-start(bf16[128,128,4]{0,2,1:T(4,128)(2,1)S(1)} %multiply_convert_fusion) | copy-start | bytes 393220
  29.4 176.2 %copy-start.43 = (bf16[128,128,4]{1,0,2:T(8,128)(2,1)}, bf16[128,128,4]{1,0,2:T(8,128)(2,1)S(1)}, u32[]{:S(2)}) copy-start(bf16[128,128,4]{1,0,2:T(8,128)(2,1)S(1)} %copy.24) | copy-start | bytes 393220
  30.9 5.2 copy-start.20
  36.0 2.4 copy-start.2
  36.0 2.4 copy-start.37
  45.6 139.9 %all-to-all-start = ((bf16[128,4,256]{2,1,0:T(4,128)(2,1)}), bf16[128,4,256]{2,1,0:T(4,128)(2,1)}, u32[]{:S(2)}, u32[]{:S(2)}) async-start(bf16[128,4,256]{2,1,0:T(4,128)(2,1)} %reshape.106), calls=%async_computation | async-start | bytes 524288 | tf_op jit(solution)/shard_map/all_to_all | solution.py:128
  129.3 1.4 copy-start.3
  130.6 2.2 copy-start.26
  138.5 1.4 copy-start.4
  139.9 2.2 copy-start.28
  147.6 1.4 copy-start.5
  149.0 2.2 copy-start.30
  156.9 1.4 copy-start.6
  158.2 2.2 copy-start.32
  166.0 1.4 copy-start.7
  167.3 2.2 copy-start.34
  175.1 1.4 copy-start.8
  176.4 2.2 copy-start.23
  183.1 2.4 copy-start.48
  189.4 16.2 %all-to-all-start.1 = ((bf16[128,4,256]{2,1,0:T(4,128)(2,1)}), bf16[128,4,256]{2,1,0:T(4,128)(2,1)}, u32[]{:S(2)}, u32[]{:S(2)}) async-start(bf16[128,4,256]{2,1,0:T(4,128)(2,1)} %copy.23), calls=%async_computation.1 | async-start | bytes 524288 | tf_op jit(solution)/shard_map/all_to_all | solution.py:126
  210.3 5.6 collective-permute-start.7
  213.0 3.7 collective-permute-start.6
  217.0 8.1 %collective-permute-start.9 = (bf16[16,34,1]{2,1,0:T(8,128)(2,1)S(1)}, bf16[16,34,1]{2,1,0:T(8,128)(2,1)S(1)}, u32[]{:S(2)}, u32[]{:S(2)}) collective-permute-start(bf16[16,34,1]{2,1,0:T(8,128)(2,1)S(1)} %get-tuple-element.106), channel_id=1, source_target_pairs={{4,0},{8,4},{12,8},{5,1},{9,5},{13,9},{6,2},{10,6},{14,10},{7,3},{... | collective-permute-start | bytes 3272 | tf_op jit(solution)/shard_map/ppermute | solution.py:22
  218.3 7.7 %collective-permute-start.8 = (bf16[16,34,1]{2,1,0:T(8,128)(2,1)S(1)}, bf16[16,34,1]{2,1,0:T(8,128)(2,1)S(1)}, u32[]{:S(2)}, u32[]{:S(2)}) collective-permute-start(bf16[16,34,1]{2,1,0:T(8,128)(2,1)S(1)} %get-tuple-element.105), channel_id=1, source_target_pairs={{0,4},{4,8},{8,12},{1,5},{5,9},{9,13},{2,6},{6,10},{10,14},{3,7},{... | collective-permute-start | bytes 3272 | tf_op jit(solution)/shard_map/ppermute | solution.py:19
  226.8 17.3 %collective-permute-start.11 = (bf16[1,34,258]{2,1,0:T(8,128)(2,1)}, bf16[1,34,258]{2,1,0:T(8,128)(2,1)S(1)}, u32[]{:S(2)}, u32[]{:S(2)}) collective-permute-start(bf16[1,34,258]{2,1,0:T(8,128)(2,1)} %get-tuple-element.98), channel_id=1, source_target_pairs={{1,0},{2,1},{3,2},{5,4},{6,5},{7,6},{9,8},{10,9},{11,10},{13,12},{... | collective-permute-start | bytes 52640 | tf_op jit(solution)/shard_map/ppermute | solution.py:22
  228.1 16.1 %collective-permute-start.10 = (bf16[1,34,258]{2,1,0:T(8,128)(2,1)}, bf16[1,34,258]{2,1,0:T(8,128)(2,1)S(1)}, u32[]{:S(2)}, u32[]{:S(2)}) collective-permute-start(bf16[1,34,258]{2,1,0:T(8,128)(2,1)} %get-tuple-element.97), channel_id=1, source_target_pairs={{0,1},{1,2},{2,3},{4,5},{5,6},{6,7},{8,9},{9,10},{10,11},{12,13},{... | collective-permute-start | bytes 52640 | tf_op jit(solution)/shard_map/ppermute | solution.py:19
  244.1 1.6 copy-start.9
  244.1 1.6 copy-start.21
  244.1 1.6 copy-start.35
  314.7 1.4 copy-start.10
  316.1 2.3 copy-start.18
  316.1 2.3 copy-start.36
  319.6 3.3 copy-start.40
  323.9 131.5 %all-to-all-start.2 = ((bf16[128,4,256]{2,1,0:T(4,128)(2,1)}), bf16[128,4,256]{2,1,0:T(4,128)(2,1)S(1)}, u32[]{:S(2)}, u32[]{:S(2)}) async-start(bf16[128,4,256]{2,1,0:T(4,128)(2,1)} %reshape.108), calls=%async_computation.2 | async-start | bytes 524288 | tf_op jit(solution)/shard_map/all_to_all | solution.py:128
  399.3 1.4 copy-start.11
  400.6 2.2 copy-start.25
  408.4 1.4 copy-start.12
  409.8 2.2 copy-start.27
  418.9 2.2 copy-start.29
  428.0 2.2 copy-start.31
  435.7 1.4 copy-start.15
  437.1 2.2 copy-start.33
  446.3 2.2 copy-start.22
  459.3 16.2 %all-to-all-start.3 = ((bf16[128,4,256]{2,1,0:T(4,128)(2,1)}), bf16[128,4,256]{2,1,0:T(4,128)(2,1)}, u32[]{:S(2)}, u32[]{:S(2)}) async-start(bf16[128,4,256]{2,1,0:T(4,128)(2,1)} %copy.27), calls=%async_computation.3 | async-start | bytes 524288 | tf_op jit(solution)/shard_map/all_to_all | solution.py:126
  464.6 10.9 %copy-start.44 = (bf16[128,128,4]{1,0,2:T(8,128)(2,1)S(1)}, bf16[128,128,4]{1,0,2:T(8,128)(2,1)}, u32[]{:S(2)}) copy-start(bf16[128,128,4]{1,0,2:T(8,128)(2,1)} %copy-done.43) | copy-start | bytes 393220
  547.8 22.8 %copy-start.38 = (f32[16,32,256]{2,1,0:T(8,128)}, f32[16,32,256]{2,1,0:T(8,128)S(1)}, u32[]{:S(2)}) copy-start(f32[16,32,256]{2,1,0:T(8,128)S(1)} %get-tuple-element.15) | copy-start | bytes 1572868
  547.9 5.8 collective-permute-start.13
  550.6 3.7 collective-permute-start.12
  554.6 8.1 %collective-permute-start.15 = (bf16[16,34,1]{2,1,0:T(8,128)(2,1)S(1)}, bf16[16,34,1]{2,1,0:T(8,128)(2,1)S(1)}, u32[]{:S(2)}, u32[]{:S(2)}) collective-permute-start(bf16[16,34,1]{2,1,0:T(8,128)(2,1)S(1)} %get-tuple-element.104), channel_id=1, source_target_pairs={{4,0},{8,4},{12,8},{5,1},{9,5},{13,9},{6,2},{10,6},{14,10},{7,3},{... | collective-permute-start | bytes 3272 | tf_op jit(solution)/shard_map/ppermute | solution.py:22
  555.9 14.7 %copy-start.17 = (f32[16,32,256]{2,1,0:T(8,128)S(1)}, f32[16,32,256]{2,1,0:T(8,128)}, u32[]{:S(2)}) copy-start(f32[16,32,256]{2,1,0:T(8,128)} %copy-done.2) | copy-start | bytes 1572868
  555.9 7.9 %collective-permute-start.14 = (bf16[16,34,1]{2,1,0:T(8,128)(2,1)S(1)}, bf16[16,34,1]{2,1,0:T(8,128)(2,1)S(1)}, u32[]{:S(2)}, u32[]{:S(2)}) collective-permute-start(bf16[16,34,1]{2,1,0:T(8,128)(2,1)S(1)} %get-tuple-element.103), channel_id=1, source_target_pairs={{0,4},{4,8},{8,12},{1,5},{5,9},{9,13},{2,6},{6,10},{10,14},{3,7},{... | collective-permute-start | bytes 3272 | tf_op jit(solution)/shard_map/ppermute | solution.py:19
  563.8 5.3 collective-permute-start.17
  565.1 5.0 collective-permute-start.16
  (7 other events, 8.2 us)
